TPU v7x, 32 devices: a whole 2x2x4 slice. The times are simulated.
32 devices in a mesh: groups: 2 (over y), dp: 4 (over z), kv: 4 (over x, core).
Axes of the slice: x: 2, y: 2, z: 4, core: 2. Of those that a mesh axis runs over, the one named last changes fastest.
Arguments:
- queries: bfloat16 [128, 3, 8192], P(('groups', 'dp'), None, 'kv'), parts along dimension 0, may hold values from -12 to 12
- routes: int32 [128, 1], P(('groups', 'dp')), parts along dimension 0, may hold values from 0 to 3; in each aligned block of 16 rows (0 to 15, 16 to 31, ...) at most 8 rows name the same one
- suffix_lengths: int32 [128], P(('groups', 'dp')), parts along dimension 0, may hold values from 128 to 256
- prefix_keys: bfloat16 [8, 2048, 1024], P(('groups', 'dp'), None, 'kv'), parts along dimension 0, may hold values from -8 to 8
- prefix_values: bfloat16 [8, 2048, 1024], P(('groups', 'dp'), None, 'kv'), parts along dimension 0, may hold values from -4.5 to 4.5
- suffix_keys: bfloat16 [128, 256, 1024], P(('groups', 'dp'), None, 'kv'), parts along dimension 0, may hold values from -4.5 to 4.5
- suffix_values: bfloat16 [128, 256, 1024], P(('groups', 'dp'), None, 'kv'), parts along dimension 0, may hold values from -4.5 to 4.5
- new_keys: bfloat16 [128, 3, 1024], P(('groups', 'dp'), None, 'kv'), parts along dimension 0, may hold values from -4.5 to 4.5
- new_values: bfloat16 [128, 3, 1024], P(('groups', 'dp'), None, 'kv'), parts along dimension 0, may hold values from -4.5 to 4.5
- out_weight: bfloat16 [8192, 8192], P('kv', 'dp'), may hold values from -0.0625 to 0.0625
Outputs:
- projected: bfloat16 [128, 3, 8192], P(('groups', 'kv'), None, 'dp'), parts along dimension 0
There are 2 independent parts, one for each index of `groups`. A program takes and returns all parts, laid end to end along the dimension named above; an argument that names none is the same for every part. Nothing has to cross between parts.
Inputs may be any that keep to these rules, and one draw needn't show every extreme that they name: `routes`: among the 16 candidates of one index of dp at most 8 continue the same prompt, and in every draw some prompt receives exactly 8 of them from some index.
All inputs are finite; a program needn't handle non-finite values.
Results may differ from a plain program's by a relative error of at most 0.008.
Values may be sent and summed in bfloat16 or wider, within the bound.
A program may use at most 128 MiB of HBM per device.

v0:
```python
import math

import jax
import jax.numpy as jnp
from jax import lax
from jax.sharding import PartitionSpec as P

HD = 128


def local(
    queries,
    routes,
    suffix_lengths,
    prefix_keys,
    prefix_values,
    suffix_keys,
    suffix_values,
    new_keys,
    new_values,
    out_weight,
):
    owners_count = lax.axis_size("dp")
    cand_count, step_count, query_width = queries.shape
    kv_width = prefix_keys.shape[2]
    kv_heads = kv_width // HD
    group_size = query_width // kv_width
    capacity = max(2, 2 * cand_count // owners_count)
    score_scale = 1.0 / math.sqrt(HD)
    owner_index = routes[:, 0]
    owner_table = (
        owner_index[:, None] == jnp.arange(owners_count, dtype=jnp.int32)[None, :]
    ).astype(jnp.int32)
    earlier_same = jnp.cumsum(owner_table, 0) - owner_table
    slot_rank = jnp.sum(earlier_same * owner_table, 1)
    slot_index = owner_index * capacity + slot_rank
    placement = (
        slot_index[None, :] == jnp.arange(owners_count * capacity, dtype=jnp.int32)[:, None]
    ).astype(jnp.bfloat16)
    outgoing = jnp.dot(
        placement,
        queries.reshape(cand_count, step_count * query_width),
        preferred_element_type=jnp.float32,
    )
    outgoing = outgoing.astype(jnp.bfloat16).reshape(
        owners_count, capacity, step_count, query_width
    )
    prompt_keys = prefix_keys[0].reshape(-1, kv_heads, HD)
    prompt_values = prefix_values[0].reshape(-1, kv_heads, HD).astype(jnp.float32)
    received = lax.all_to_all(outgoing, "dp", split_axis=0, concat_axis=0, tiled=True)
    row_shape = received.shape
    query_heads = received.reshape(-1, kv_heads, group_size, HD)
    scores = (
        jnp.einsum("rhgd,khd->rhgk", query_heads, prompt_keys, preferred_element_type=jnp.float32)
        * score_scale
    )
    peak_score = jnp.max(scores, -1, keepdims=True)
    weights = jnp.exp(scores - peak_score)
    weight_sum = jnp.sum(weights, -1, keepdims=True)
    combined = jnp.einsum("rhgk,khd->rhgd", weights, prompt_values) / weight_sum
    log_total = (peak_score + jnp.log(weight_sum))[..., 0]
    homeward = (
        lax.all_to_all(combined.reshape(row_shape), "dp", split_axis=0, concat_axis=0, tiled=True),
        lax.all_to_all(
            log_total.reshape(row_shape[0], row_shape[1], row_shape[2], kv_heads * group_size),
            "dp",
            split_axis=0,
            concat_axis=0,
            tiled=True,
        ),
    )
    prompt_rows = homeward[0]
    prompt_totals = homeward[1]
    prompt_rows = jnp.take(
        prompt_rows.reshape(owners_count * capacity, step_count, query_width), slot_index, axis=0
    )
    prompt_totals = jnp.take(
        prompt_totals.reshape(owners_count * capacity, step_count, kv_heads * group_size),
        slot_index,
        axis=0,
    )
    query_heads = queries.reshape(cand_count, step_count, kv_heads, group_size, HD)
    cache_keys = suffix_keys.reshape(cand_count, -1, kv_heads, HD)
    cache_length = cache_keys.shape[1]
    cache_scores = jnp.einsum(
        "cshgd,cjhd->cshgj", query_heads, cache_keys, preferred_element_type=jnp.float32
    )
    fresh_scores = jnp.einsum(
        "cshgd,cthd->cshgt",
        query_heads,
        new_keys.reshape(cand_count, step_count, kv_heads, HD),
        preferred_element_type=jnp.float32,
    )
    scores = jnp.concatenate([cache_scores, fresh_scores], -1) * score_scale
    cache_allowed = jnp.arange(cache_length, dtype=jnp.int32)[None, :] < suffix_lengths[:, None]
    step_positions = jnp.arange(step_count, dtype=jnp.int32)
    fresh_allowed = step_positions[None, :] <= step_positions[:, None]
    allowed = jnp.concatenate(
        [
            jnp.broadcast_to(cache_allowed[:, None, :], (cand_count, step_count, cache_length)),
            jnp.broadcast_to(fresh_allowed[None, :, :], (cand_count, step_count, step_count)),
        ],
        -1,
    )
    scores = jnp.where(allowed[:, :, None, None, :], scores, -jnp.inf)
    peak_score = jnp.max(scores, -1, keepdims=True)
    weights = jnp.exp(scores - peak_score)
    weight_sum = jnp.sum(weights, -1, keepdims=True)
    value_rows = jnp.concatenate(
        [
            suffix_values.reshape(cand_count, -1, kv_heads, HD),
            new_values.reshape(cand_count, step_count, kv_heads, HD),
        ],
        1,
    ).astype(jnp.float32)
    suffix_rows = jnp.einsum("cshgj,cjhd->cshgd", weights, value_rows) / weight_sum
    suffix_totals = (peak_score + jnp.log(weight_sum))[..., 0]
    prompt_rows = prompt_rows.reshape(cand_count, step_count, kv_heads, group_size, HD)
    prompt_totals = prompt_totals.reshape(cand_count, step_count, kv_heads, group_size)
    common_peak = jnp.maximum(prompt_totals, suffix_totals)
    prompt_share = jnp.exp(prompt_totals - common_peak)[..., None]
    suffix_share = jnp.exp(suffix_totals - common_peak)[..., None]
    attended = (prompt_share * prompt_rows + suffix_share * suffix_rows) / (
        prompt_share + suffix_share
    )
    attended = attended.reshape(cand_count, step_count, query_width).astype(jnp.bfloat16)
    block_rows = lax.all_gather(attended, "dp", axis=0, tiled=True)
    row_count = block_rows.shape[0]
    product = jnp.dot(
        block_rows.reshape(-1, query_width), out_weight, preferred_element_type=jnp.float32
    )
    partial_value = product.reshape(row_count, step_count, -1)
    return lax.psum_scatter(partial_value, "kv", scatter_dimension=0, tiled=True).astype(
        jnp.bfloat16
    )


def solution(mesh):
    placed = (
        P(("groups", "dp"), None, "kv"),
        P(("groups", "dp"), None),
        P(("groups", "dp")),
        P(("groups", "dp"), None, "kv"),
        P(("groups", "dp"), None, "kv"),
        P(("groups", "dp"), None, "kv"),
        P(("groups", "dp"), None, "kv"),
        P(("groups", "dp"), None, "kv"),
        P(("groups", "dp"), None, "kv"),
        P("kv", "dp"),
    )
    return jax.shard_map(
        local,
        mesh=mesh,
        in_specs=placed,
        out_specs=P(("groups", "kv"), None, "dp"),
        check_vma=False,
    )
```

profile of v0, /device:TPU:0, one launch (start us, length us, event | category | flops | bytes accessed | tf_op | source)
XLA Modules:
  0.0 142.7 jit_solution(114557513929737650)
XLA Ops:
  6.5 0.8 fusion.46
  7.4 0.8 select_reduce_fusion
  8.2 0.7 multiply_add_fusion
  8.9 0.9 copy.132
  9.8 1.0 convolution_convert_fusion
  10.8 6.3 %all-to-all-start = ((bf16[4,8,3,2048]{3,1,2,0:T(8,128)(2,1)}), bf16[4,8,3,2048]{3,1,2,0:T(8,128)(2,1)S(1)}, u32[]{:S(2)}, u32[]{:S(2)}) async-start(bf16[4,8,3,2048]{3,1,2,0:T(8,128)(2,1)} %bitcast.3), calls=%async_computation | async-start | bytes 786432 | tf_op jit(solution)/shard_map/all_to_all | solution.py:50
  17.2 0.0 copy-done.1
  17.2 0.0 copy-start.7
  17.2 0.0 copy-start.6
  17.2 0.3 reshape_squeeze.7
  17.5 1.3 reshape_squeeze.8
  18.9 0.0 copy-done.7
  18.9 0.1 iota_compare_fusion
  19.0 0.6 pad_add_fusion
  19.6 0.0 copy-done.6
  19.6 9.2 %all-to-all-done = bf16[4,8,3,2048]{3,1,2,0:T(8,128)(2,1)S(1)} async-done(((bf16[4,8,3,2048]{3,1,2,0:T(8,128)(2,1)}), bf16[4,8,3,2048]{3,1,2,0:T(8,128)(2,1)S(1)}, u32[]{:S(2)}, u32[]{:S(2)}) %all-to-all-start) | async-done | bytes 393248 | tf_op jit(solution)/shard_map/all_to_all | solution.py:50
  28.8 0.3 copy.91
  29.2 0.5 reshape.137
  29.7 6.4 %bitcast_reduce_fusion = (f32[96,2,8]{2,0,1:T(8,128)S(1)}, f32[2,96,8,2048]{3,2,1,0:T(8,128)}) fusion(bf16[2048,2,128,1]{2,1,0,3:T(2,128)(2,1)S(1)} %bitcast.96, bf16[96,2,8,128]{3,2,1,0:T(8,128)(2,1)S(1)} %reshape.137), kind=kOutput, calls=%fused_computation.3 | convolution fusion | flops 811596288 | bytes 14030848 | tf_op jit(solution)/shard_map/rhgd,khd->rhgk/dot_general | solution.py:54
  36.0 0.1 copy.95
  36.1 6.1 %fusion.3 = f32[96,2,8]{2,0,1:T(8,128)S(1)} fusion(f32[2,96,8,2048]{3,2,1,0:T(8,128)} %get-tuple-element.11, f32[96,2,8]{2,0,1:T(8,128)S(1)} %get-tuple-element.10), kind=kLoop, calls=%fused_computation.6 | loop fusion | flops 9435648 | bytes 12595200 | tf_op jit(solution)/shard_map/reduce_sum | solution.py:59
  42.2 0.1 copy.94
  42.3 0.1 copy.96
  42.5 0.1 add.61
  42.6 0.7 reshape.169
  43.3 3.2 %all-to-all-start.1 = ((f32[4,1,384]{2,1,0:T(1,128)}), f32[4,1,384]{2,1,0:T(1,128)S(1)}, u32[]{:S(2)}, u32[]{:S(2)}) async-start(f32[4,1,384]{2,1,0:T(1,128)} %reshape.169), calls=%async_computation.1 | async-start | bytes 12288 | tf_op jit(solution)/shard_map/all_to_all | solution.py:64
  46.5 5.7 %fusion.30 = f32[96,2,8,128]{3,2,0,1:T(8,128)S(1)} fusion(bf16[2048,2,128,1]{2,1,0,3:T(2,128)(2,1)S(1)} %bitcast.99, f32[2,96,8,2048]{3,2,1,0:T(8,128)} %get-tuple-element.11, f32[96,2,8]{2,0,1:T(8,128)S(1)} %get-tuple-element.10, f32[96,2,8]{2,0,1:T(8,128)S(1)} %fusion.3), kind=kOutput, calls=%fused_computation.34 | convolution fusion | flops 811794432 | bytes 14430208 | tf_op jit(solution)/shard_map/rhgk,khd->rhgd/dot_general | solution.py:60
  52.3 0.1 copy.107
  52.3 0.3 reshape.142
  52.6 0.0 copy-start.2
  52.7 0.0 copy-start
  52.7 1.3 copy.108
  54.0 0.0 all-to-all-done.1
  54.0 5.0 %all-to-all-start.2 = ((f32[4,8,3,2048]{3,1,2,0:T(8,128)}), f32[4,8,3,2048]{3,1,2,0:T(8,128)S(1)}, u32[]{:S(2)}, u32[]{:S(2)}) async-start(f32[4,8,3,2048]{3,1,2,0:T(8,128)} %copy.108), calls=%async_computation.2 | async-start | bytes 1572864 | tf_op jit(solution)/shard_map/all_to_all | solution.py:63
  59.1 0.0 reduce-scatter.2.cloned.1.call-start
  59.1 0.0 copy-done.2
  59.1 0.0 copy-done
  59.1 0.0 copy-start.4
  59.1 2.1 %reshape.139 = bf16[16,256,2,128]{3,2,1,0:T(2,128)(2,1)} reshape(bf16[16,256,256]{2,1,0:T(8,128)(2,1)S(1)} %copy-done) | data formatting | bytes 4194304 | tf_op jit(solution)/shard_map/reshape | solution.py:83
  61.2 2.9 %copy.112 = bf16[16,256,256]{1,2,0:T(8,128)(2,1)S(1)} copy(bf16[16,256,256]{2,1,0:T(8,128)(2,1)} %param.16) | data formatting | bytes 4194304 | tf_op args[6]
  64.1 0.0 copy-start.5
  64.1 2.4 %copy.113 = bf16[16,256,2,128]{3,1,2,0:T(8,128)(2,1)} copy(bf16[16,256,2,128]{1,3,2,0:T(8,128)(2,1)S(1)} %bitcast.95) | data formatting | bytes 4194304 | tf_op jit(solution)/shard_map/reshape | solution.py:111
  66.5 0.2 convolution_bitcast_fusion
  66.8 2.2 %fusion.16 = f32[16,3,2,8,256]{4,3,1,2,0:T(8,128)S(1)} fusion(bf16[16,256,2,128,1]{3,2,1,0,4:T(2,128)(2,1)} %bitcast.98, bf16[16,3,2,8,128]{4,3,2,0,1:T(8,128)(2,1)S(1)} %bitcast.101), kind=kOutput, calls=%fused_computation.19 | convolution fusion | flops 50331648 | bytes 3080192 | tf_op jit(solution)/shard_map/cshgd,cjhd->cshgj/dot_general | solution.py:85
  69.0 0.3 fusion.37
  69.3 0.5 fusion.29
  69.8 0.5 broadcast.96
  70.3 0.7 reduce
  71.0 0.1 reshape.170
  71.1 0.6 gather_fusion
  71.7 0.1 copy.99
  71.8 0.1 copy.100
  71.9 0.7 fusion.51
  72.7 5.5 %all-to-all-done.2 = f32[4,8,3,2048]{3,1,2,0:T(8,128)S(1)} async-done(((f32[4,8,3,2048]{3,1,2,0:T(8,128)}), f32[4,8,3,2048]{3,1,2,0:T(8,128)S(1)}, u32[]{:S(2)}, u32[]{:S(2)}) %all-to-all-start.2) | async-done | bytes 786464 | tf_op jit(solution)/shard_map/all_to_all | solution.py:63
  78.2 0.5 copy.109
  78.7 0.9 gather_fusion.1
  79.6 0.3 reshape.168
  79.9 2.3 %fusion.28 = bf16[16,3,2,8,128]{4,3,1,2,0:T(8,128)(2,1)S(1)} fusion(bf16[16,3,2,128]{3,1,2,0:T(4,128)(2,1)S(1)} %copy.114, bf16[16,256,2,128]{3,1,2,0:T(8,128)(2,1)} %copy.113, f32[16,3,2,8]{3,1,2,0:T(4,128)S(1)} %fusion.37, f32[16,3,2,8,3]{4,3,1,2,0:T(8,128)S(1)} %convolution_bitcast_fusion, f32[16,3,2,8,256]{4,3,1,2,0:T(8,128)S(1)} %fusion.16, ...), kind=kOutput, calls=%fused_computation.32 | convolution fusion | flops 56648704 | bytes 3535008 | tf_op jit(solution)/shard_map/cshgj,cjhd->cshgd/dot_general | solution.py:116
  82.2 0.1 convert_element_type.21
  82.3 17.7 %all_gather.3 = bf16[64,3,2048]{2,0,1:T(8,128)(2,1)S(1)} all-gather(bf16[16,3,2048]{2,0,1:T(8,128)(2,1)S(1)} %convert_element_type.21), channel_id=1, replica_groups=mesh['groups'=2,'dp'=4,'kv'=4] {'dp'}, dimensions={0}, use_global_device_ids=true | all-gather | bytes 983040 | tf_op jit(solution)/shard_map/all_gather | solution.py:127
  100.0 6.4 %fusion.4 = f32[64,3,2048]{2,0,1:T(8,128)} fusion(bf16[64,3,2048]{2,0,1:T(8,128)(2,1)S(1)} %all_gather.3, bf16[2048,2048]{1,0:T(8,128)(2,1)} %param.19), kind=kOutput, calls=%fused_computation.7 | convolution fusion | flops 1610612736 | bytes 10747904 | tf_op jit(solution)/shard_map/dot_general | solution.py:129
  106.4 0.0 reduce-scatter.2.cloned.1.call-update
  106.4 27.8 %reduce-scatter.2.cloned.1.call-done = f32[16,3,2048]{2,0,1:T(8,128)} async-done(((f32[64,3,2048]{2,0,1:T(8,128)}), f32[16,3,2048]{2,0,1:T(8,128)}) %reduce-scatter.2.cloned.1.call-update) | async-done | bytes 393232 | tf_op jit(solution)/shard_map/reduce_scatter | solution.py:133
  134.2 1.7 %convert_element_type.22 = bf16[16,3,2048]{2,0,1:T(8,128)(2,1)} convert(f32[16,3,2048]{2,0,1:T(8,128)} %reduce-scatter.2.cloned.1.call-done) | non-fusion elementwise | flops 98304 | bytes 589824 | tf_op jit(solution)/shard_map/convert_element_type | solution.py:133
  (19 shorter events, 0.2 us)
Async XLA Ops:
  6.5 10.6 %copy-start.1 = (bf16[1,2048,256]{2,1,0:T(8,128)(2,1)S(1)}, bf16[1,2048,256]{2,1,0:T(8,128)(2,1)}, u32[]{:S(2)}) copy-start(bf16[1,2048,256]{2,1,0:T(8,128)(2,1)} %param.13) | copy-start | bytes 3145732
  10.8 18.0 %all-to-all-start = ((bf16[4,8,3,2048]{3,1,2,0:T(8,128)(2,1)}), bf16[4,8,3,2048]{3,1,2,0:T(8,128)(2,1)S(1)}, u32[]{:S(2)}, u32[]{:S(2)}) async-start(bf16[4,8,3,2048]{3,1,2,0:T(8,128)(2,1)} %bitcast.3), calls=%async_computation | async-start | bytes 786432 | tf_op jit(solution)/shard_map/all_to_all | solution.py:50
  17.2 1.7 %copy-start.7 = (s32[16]{0:T(128)S(1)}, s32[16]{0:T(128)}, u32[]{:S(2)}) copy-start(s32[16]{0:T(128)} %param.12) | copy-start | bytes 196
  17.2 2.4 %copy-start.6 = (s32[16,1]{0,1:T(1,128)S(1)}, s32[16,1]{0,1:T(1,128)}, u32[]{:S(2)}) copy-start(s32[16,1]{0,1:T(1,128)} %param.11) | copy-start | bytes 196
  43.3 10.7 %all-to-all-start.1 = ((f32[4,1,384]{2,1,0:T(1,128)}), f32[4,1,384]{2,1,0:T(1,128)S(1)}, u32[]{:S(2)}, u32[]{:S(2)}) async-start(f32[4,1,384]{2,1,0:T(1,128)} %reshape.169), calls=%async_computation.1 | async-start | bytes 12288 | tf_op jit(solution)/shard_map/all_to_all | solution.py:64
  52.6 6.4 %copy-start.2 = (bf16[16,3,2048]{2,0,1:T(8,128)(2,1)S(1)}, bf16[16,3,2048]{2,0,1:T(8,128)(2,1)}, u32[]{:S(2)}) copy-start(bf16[16,3,2048]{2,0,1:T(8,128)(2,1)} %param.10) | copy-start | bytes 589828
  52.7 6.5 %copy-start = (bf16[16,256,256]{2,1,0:T(8,128)(2,1)S(1)}, bf16[16,256,256]{2,1,0:T(8,128)(2,1)}, u32[]{:S(2)}) copy-start(bf16[16,256,256]{2,1,0:T(8,128)(2,1)} %param.15) | copy-start | bytes 6291460
  54.0 24.2 %all-to-all-start.2 = ((f32[4,8,3,2048]{3,1,2,0:T(8,128)}), f32[4,8,3,2048]{3,1,2,0:T(8,128)S(1)}, u32[]{:S(2)}, u32[]{:S(2)}) async-start(f32[4,8,3,2048]{3,1,2,0:T(8,128)} %copy.108), calls=%async_computation.2 | async-start | bytes 1572864 | tf_op jit(solution)/shard_map/all_to_all | solution.py:63
  59.1 75.1 %reduce-scatter.2.cloned.1.call-start = ((), (), s32[]{:S(2)}) async-start(), calls=%async_computation.4 | async-start | bytes 1966080 | tf_op jit(solution)/shard_map/reduce_scatter | solution.py:133
  59.1 2.1 %copy-start.4 = (bf16[16,3,256]{2,0,1:T(8,128)(2,1)S(1)}, bf16[16,3,256]{2,0,1:T(8,128)(2,1)}, u32[]{:S(2)}) copy-start(bf16[16,3,256]{2,0,1:T(8,128)(2,1)} %param.17) | copy-start | bytes 73732
  64.1 2.4 %copy-start.5 = (bf16[16,3,256]{2,0,1:T(8,128)(2,1)S(1)}, bf16[16,3,256]{2,0,1:T(8,128)(2,1)}, u32[]{:S(2)}) copy-start(bf16[16,3,256]{2,0,1:T(8,128)(2,1)} %param.18) | copy-start | bytes 73732
  66.5 2.5 %copy-start.3 = (pred[16,3,259]{2,1,0:T(4,128)(4,1)S(1)}, pred[16,3,259]{2,1,0:T(4,128)(4,1)}, u32[]{:S(2)}) copy-start(pred[16,3,259]{2,1,0:T(4,128)(4,1)} %pad_add_fusion) | copy-start | bytes 37300
Sparse Core Ops, SparseCore 0:
  106.5 27.5 reduce-scatter.1
where the time goes:
time: 143 us
  waiting for transfers between devices  42.5 us (30%)
  matrix products  24.2 us (17%)
  blocking collectives  17.7 us (12%)
  local copies, waits for them, and re-layouts  16.8 us (12%)
  starting transfers between devices  14.6 us (10%)
  between operations  13.7 us (10%)
  other arithmetic  13.2 us (9%)
    reduce_scatter x1, waiting for transfers between devices, local(): lax.psum_scatter(partial_value, 'kv', scatter_dimension=0, tiled=True)  27.8 us
    all_gather x1, blocking collectives, local(): block_rows = lax.all_gather(attended, 'dp', axis=0, tiled=True)  17.7 us
    all_to_all x1, waiting for transfers between devices, local(): lax.all_to_all(outgoing, 'dp', split_axis=0, concat_axis=0, tiled=True)  9.21 us
    reduce_sum x2, other arithmetic, local(): weight_sum = jnp.sum(weights, -1, keepdims=True)  6.66 us
    dot_general x1, matrix products, local(): jnp.einsum('rhgd,khd->rhgk', query_heads, prompt_keys, preferred_element_...  6.38 us
    dot_general x1, matrix products, local(): jnp.dot(block_rows.reshape(-1, query_width), out_weight, preferred_elemen...  6.36 us
    all_to_all x1, starting transfers between devices, local(): lax.all_to_all(outgoing, 'dp', split_axis=0, concat_axis=0, tiled=True)  6.35 us
    dot_general x1, matrix products, local(): combined = jnp.einsum('rhgk,khd->rhgd', weights, prompt_values) / weight_sum  5.72 us
  transfers between devices with their start and end apart: 4, of which 3 were waited for; matrix products, arithmetic and copies ran while one was open for 16% of the time, Pallas kernels for 0%

commit v1 on v0

v1 whole, which is shorter than its diff:
```python
import functools
import math

import jax
import jax.numpy as jnp
from jax import lax
from jax.experimental import pallas as pl
from jax.experimental.pallas import tpu as pltpu
from jax.sharding import PartitionSpec as P

HD = 128
MESH = pl.DeviceIdType.MESH
NEG = -1e30


def kernel(
    n,
    n_kv,
    cap,
    slot_ref,
    inv_ref,
    len_ref,
    q_ref,
    nk_ref,
    nv_ref,
    pk_hbm,
    pv_hbm,
    sk_hbm,
    sv_hbm,
    w_hbm,
    o_ref,
    kbuf,
    vbuf,
    skbuf,
    svbuf,
    wbuf,
    qsend,
    qrecv,
    suf_o,
    suf_l,
    psend_o,
    psend_l,
    precv_o,
    precv_l,
    att,
    gath,
    ysend,
    red,
    own,
    local_sem,
    q_ss,
    q_rs,
    po_ss,
    po_rs,
    pl_ss,
    pl_rs,
    g_ss,
    g_rs,
    y_ss,
    y_rs,
):
    f32, bf16 = jnp.float32, jnp.bfloat16
    me = lax.axis_index("dp")
    kv = lax.axis_index("kv")
    cands, steps, heads, _ = q_ref.shape
    kv_heads = kbuf.shape[1] // HD
    group = heads // kv_heads
    rows = cands * steps
    gc = n // n_kv
    cols = wbuf.shape[1]
    scale = 1.0 / math.sqrt(HD)

    loads = [
        pltpu.make_async_copy(src, dst, local_sem.at[i])
        for i, (src, dst) in enumerate(
            [(sk_hbm, skbuf), (sv_hbm, svbuf), (pk_hbm, kbuf), (pv_hbm, vbuf), (w_hbm, wbuf)]
        )
    ]
    for load in loads:
        load.start()

    barrier = pltpu.get_barrier_semaphore()

    @pl.loop(1, n)
    def _(k):
        pl.semaphore_signal(
            barrier, inc=1, device_id={"dp": lax.rem(me + k, n)}, device_id_type=MESH
        )

    @pl.loop(1, n_kv)
    def _(k):
        pl.semaphore_signal(
            barrier, inc=1, device_id={"kv": lax.rem(kv + k, n_kv)}, device_id_type=MESH
        )

    @pl.loop(0, n)
    def _(k):
        for j in range(cap):
            qsend[k, j] = q_ref[inv_ref[k * cap + j]]

    qrecv[0] = qsend[0]
    pl.semaphore_wait(barrier, n - 1 + n_kv - 1)

    def q_copy(k):
        return pltpu.make_async_remote_copy(
            src_ref=qsend.at[k],
            dst_ref=qrecv.at[k],
            send_sem=q_ss.at[k],
            recv_sem=q_rs.at[k],
            device_id={"dp": lax.rem(me + k, n)},
            device_id_type=MESH,
        )

    def po_copy(k):
        return pltpu.make_async_remote_copy(
            src_ref=psend_o.at[k],
            dst_ref=precv_o.at[pl.ds(k * cap, cap)],
            send_sem=po_ss.at[k],
            recv_sem=po_rs.at[k],
            device_id={"dp": lax.rem(me + n - k, n)},
            device_id_type=MESH,
        )

    def pl_copy(k):
        return pltpu.make_async_remote_copy(
            src_ref=psend_l.at[k],
            dst_ref=precv_l.at[pl.ds(k * cap, cap)],
            send_sem=pl_ss.at[k],
            recv_sem=pl_rs.at[k],
            device_id={"dp": lax.rem(me + n - k, n)},
            device_id_type=MESH,
        )

    def g_copy(k):
        return pltpu.make_async_remote_copy(
            src_ref=gath.at[0],
            dst_ref=gath.at[k],
            send_sem=g_ss.at[k],
            recv_sem=g_rs.at[k],
            device_id={"dp": lax.rem(me + k, n)},
            device_id_type=MESH,
        )

    @pl.loop(1, n)
    def _(k):
        q_copy(k).start()

    loads[0].wait()
    loads[1].wait()
    depth = skbuf.shape[1]
    position = lax.broadcasted_iota(jnp.int32, (steps * group, depth), 1)
    step_of = lax.broadcasted_iota(jnp.int32, (steps, group, 1), 0).reshape(steps * group, 1)

    def suffix(c):
        q = q_ref[c].astype(f32)
        fresh_k = nk_ref[c].astype(f32)
        fresh_v = nv_ref[c].astype(f32)
        length = len_ref[c]
        outs, totals = [], []
        for h in range(kv_heads):
            lanes = slice(h * HD, (h + 1) * HD)
            qh = q[:, h * group : (h + 1) * group, :].reshape(steps * group, HD)
            s = lax.dot_general(
                qh.astype(bf16),
                skbuf[c, :, lanes],
                (((1,), (1,)), ((), ())),
                preferred_element_type=f32,
            )
            s = jnp.where(position < length, s * scale, NEG)
            top = jnp.max(s, 1, keepdims=True)
            news = []
            for t in range(steps):
                f = jnp.sum(qh * fresh_k[t : t + 1, lanes], 1, keepdims=True) * scale
                f = jnp.where(step_of >= t, f, NEG)
                top = jnp.maximum(top, f)
                news.append(f)
            p = jnp.exp(s - top)
            total = jnp.sum(p, 1, keepdims=True)
            o = jnp.dot(p.astype(bf16), svbuf[c, :, lanes], preferred_element_type=f32)
            for t in range(steps):
                e = jnp.exp(news[t] - top)
                total = total + e
                o = o + e * fresh_v[t : t + 1, lanes]
            outs.append((o / total).reshape(steps, group, HD))
            totals.append(
                jnp.broadcast_to(top + jnp.log(total), (steps * group, HD)).reshape(
                    steps, group, HD
                )
            )
        suf_o[c] = jnp.concatenate(outs, 1)
        suf_l[c] = jnp.concatenate(totals, 1)

    together = 4 if cands % 4 == 0 else 1

    @pl.loop(0, cands // together)
    def _(i):
        for u in range(together):
            suffix(i * together + u)

    loads[2].wait()
    loads[3].wait()
    lane = lax.broadcasted_iota(jnp.int32, (1, group, HD), 2)
    sub = lax.broadcasted_iota(jnp.int32, (1, group, HD), 1)

    @pl.loop(0, n)
    def _(k):
        @pl.when(k > 0)
        def _():
            q_copy(k).wait_recv()

        x = qrecv[k].astype(f32).reshape(cap * steps, heads, HD)
        outs, packed = [], None
        for h in range(kv_heads):
            lanes = slice(h * HD, (h + 1) * HD)
            xh = x[:, h * group : (h + 1) * group, :].reshape(cap * steps * group, HD)
            s = (
                lax.dot_general(
                    xh.astype(bf16),
                    kbuf[:, lanes],
                    (((1,), (1,)), ((), ())),
                    preferred_element_type=f32,
                )
                * scale
            )
            top = jnp.max(s, 1, keepdims=True)
            p = jnp.exp(s - top)
            total = jnp.sum(p, 1, keepdims=True)
            o = jnp.dot(p.astype(bf16), vbuf[:, lanes], preferred_element_type=f32) / total
            outs.append(o.reshape(cap * steps, group, HD))
            lse = jnp.broadcast_to(top + jnp.log(total), (cap * steps * group, HD))
            lse = lse.reshape(cap * steps, group, HD)
            lse = jnp.sum(jnp.where(lane == sub + h * group, lse, 0.0), 1)
            packed = lse if packed is None else packed + lse
        o = jnp.concatenate(outs, 1).astype(bf16).reshape(cap, steps, heads, HD)
        packed = packed.reshape(cap, steps, HD)

        @pl.when(k == 0)
        def _():
            precv_o[0:cap] = o
            precv_l[0:cap] = packed

        @pl.when(k > 0)
        def _():
            psend_o[k] = o
            psend_l[k] = packed
            po_copy(k).start()
            pl_copy(k).start()

    @pl.loop(1, n)
    def _(k):
        po_copy(k).wait_recv()
        pl_copy(k).wait_recv()

    diag = lax.broadcasted_iota(jnp.int32, (steps, heads, HD), 2) == lax.broadcasted_iota(
        jnp.int32, (steps, heads, HD), 1
    )

    @pl.loop(0, cands)
    def _(c):
        slot = slot_ref[c]
        pr = precv_o[slot].astype(f32)
        pt = jnp.broadcast_to(precv_l[slot].reshape(steps, 1, HD), (steps, heads, HD))
        pt = jnp.sum(jnp.where(diag, pt, 0.0), 2, keepdims=True)
        st = suf_l[c]
        peak = jnp.maximum(pt, st)
        a = jnp.exp(pt - peak)
        b = jnp.exp(st - peak)
        merged = (a * pr + b * suf_o[c]) / (a + b)
        att[pl.ds(pl.multiple_of(c * steps * heads, 8), steps * heads), :] = merged.reshape(
            steps * heads, HD
        )

    for hg in range(heads):
        gath[0, :, hg * HD : (hg + 1) * HD] = att[pl.ds(hg, rows, stride=heads), :].astype(bf16)

    @pl.loop(1, n)
    def _(k):
        g_copy(k).start()

    loads[4].wait()
    tile = min(512, cols)

    def y_copy(k):
        src = lax.rem(me + n - k, n)
        to = src // gc
        j = lax.rem(to + n_kv - kv, n_kv)
        pos = lax.rem(src, gc)
        return j, pos, pltpu.make_async_remote_copy(
            src_ref=ysend.at[k],
            dst_ref=red.at[j, pos],
            send_sem=y_ss.at[k],
            recv_sem=y_rs.at[j * gc + pos],
            device_id={"kv": to},
            device_id_type=MESH,
        )

    @pl.loop(0, n)
    def _(k):
        @pl.when(k > 0)
        def _():
            g_copy(k).wait_recv()

        j, pos, copy = y_copy(k)

        @pl.loop(0, cols // tile)
        def _(t):
            at = pl.ds(pl.multiple_of(t * tile, 128), tile)
            y = jnp.dot(gath[k], wbuf[:, at], preferred_element_type=f32)

            @pl.when(j == 0)
            def _():
                own[pos, :, at] = y

            @pl.when(j > 0)
            def _():
                ysend[k, :, at] = y.astype(bf16)

        @pl.when(j > 0)
        def _():
            copy.start()

    @pl.loop(0, gc)
    def _(pos):
        total = own[pos]
        for j in range(1, n_kv):
            pltpu.make_async_remote_copy(
                src_ref=ysend.at[0],
                dst_ref=red.at[j, pos],
                send_sem=y_ss.at[0],
                recv_sem=y_rs.at[j * gc + pos],
                device_id={"kv": lax.rem(kv + j, n_kv)},
                device_id_type=MESH,
            ).wait_recv()
            total = total + red[j, pos].astype(f32)
        o_ref[pos] = total.astype(bf16)

    @pl.loop(1, n)
    def _(k):
        q_copy(k).wait_send()
        po_copy(k).wait_send()
        pl_copy(k).wait_send()
        g_copy(k).wait_send()

    @pl.loop(0, n)
    def _(k):
        j, pos, copy = y_copy(k)

        @pl.when(j > 0)
        def _():
            copy.wait_send()


def local(
    queries,
    routes,
    suffix_lengths,
    prefix_keys,
    prefix_values,
    suffix_keys,
    suffix_values,
    new_keys,
    new_values,
    out_weight,
):
    n = lax.axis_size("dp")
    n_kv = lax.axis_size("kv")
    cands, steps, query_width = queries.shape
    kv_width = prefix_keys.shape[2]
    plen = prefix_keys.shape[1]
    depth = suffix_keys.shape[1]
    cols = out_weight.shape[1]
    heads = query_width // HD
    rows = cands * steps
    gc = n // n_kv
    cap = max(2, 2 * cands // n)
    me = lax.axis_index("dp")
    away = lax.rem(routes[:, 0] - me + n, n)
    order = jnp.arange(cands, dtype=jnp.int32)
    earlier = (away[:, None] == away[None, :]) & (order[None, :] < order[:, None])
    slot = away * cap + jnp.sum(earlier.astype(jnp.int32), 1)
    places = jnp.arange(n * cap, dtype=jnp.int32)
    inverse = jnp.sum(jnp.where(slot[None, :] == places[:, None], order[None, :], 0), 1)
    bf16, f32 = jnp.bfloat16, jnp.float32
    smem = pl.BlockSpec(memory_space=pltpu.SMEM)
    vmem = pl.BlockSpec(memory_space=pltpu.VMEM)
    hbm = pl.BlockSpec(memory_space=pl.ANY)
    dma = pltpu.SemaphoreType.DMA
    out = pl.pallas_call(
        functools.partial(kernel, n, n_kv, cap),
        out_shape=jax.ShapeDtypeStruct((gc, rows, cols), bf16),
        in_specs=[smem] * 3 + [vmem] * 3 + [hbm] * 5,
        out_specs=vmem,
        scratch_shapes=[
            pltpu.VMEM((plen, kv_width), bf16),
            pltpu.VMEM((plen, kv_width), bf16),
            pltpu.VMEM((cands, depth, kv_width), bf16),
            pltpu.VMEM((cands, depth, kv_width), bf16),
            pltpu.VMEM((query_width, cols), bf16),
            pltpu.VMEM((n, cap, steps, heads, HD), bf16),
            pltpu.VMEM((n, cap, steps, heads, HD), bf16),
            pltpu.VMEM((cands, steps, heads, HD), f32),
            pltpu.VMEM((cands, steps, heads, HD), f32),
            pltpu.VMEM((n, cap, steps, heads, HD), bf16),
            pltpu.VMEM((n, cap, steps, HD), f32),
            pltpu.VMEM((n * cap, steps, heads, HD), bf16),
            pltpu.VMEM((n * cap, steps, HD), f32),
            pltpu.VMEM((rows * heads, HD), f32),
            pltpu.VMEM((n, rows, query_width), bf16),
            pltpu.VMEM((n, rows, cols), bf16),
            pltpu.VMEM((n_kv, gc, rows, cols), bf16),
            pltpu.VMEM((gc, rows, cols), f32),
            dma((5,)),
            dma((n,)),
            dma((n,)),
            dma((n,)),
            dma((n,)),
            dma((n,)),
            dma((n,)),
            dma((n,)),
            dma((n,)),
            dma((n,)),
            dma((n_kv * gc,)),
        ],
        compiler_params=pltpu.CompilerParams(
            collective_id=0, has_side_effects=True, vmem_limit_bytes=60 * 1024 * 1024
        ),
    )(
        slot,
        inverse,
        suffix_lengths,
        queries.reshape(cands, steps, heads, HD),
        new_keys,
        new_values,
        prefix_keys[0],
        prefix_values[0],
        suffix_keys,
        suffix_values,
        out_weight,
    )
    return out.reshape(gc * cands, steps, cols)


def solution(mesh):
    placed = (
        P(("groups", "dp"), None, "kv"),
        P(("groups", "dp"), None),
        P(("groups", "dp")),
        P(("groups", "dp"), None, "kv"),
        P(("groups", "dp"), None, "kv"),
        P(("groups", "dp"), None, "kv"),
        P(("groups", "dp"), None, "kv"),
        P(("groups", "dp"), None, "kv"),
        P(("groups", "dp"), None, "kv"),
        P("kv", "dp"),
    )
    return jax.shard_map(
        local,
        mesh=mesh,
        in_specs=placed,
        out_specs=P(("groups", "kv"), None, "dp"),
        check_vma=False,
    )
```

time: 143 us -> 64.9 us (0.45)
  the two profiles are of different devices: /device:TPU:0 before, /device:TPU:1 now
where the time goes in v1:
time: 64.9 us; the launch traced here: 64.5 us
  Pallas kernels  55.5 us (86%)
  local copies, waits for them, and re-layouts  6.24 us (10%)
  other arithmetic  2.8 us (4%)
    pallas_call x1, Pallas kernels, local(): pl.pallas_call(functools.partial(kernel, n, n_kv, cap), out_shape=jax.Sha...  55.5 us
    unnamed x5, local copies, waits for them, and re-layouts  3.67 us
    reshape x2, local copies, waits for them, and re-layouts, local(): return out.reshape(gc * cands, steps, cols)  1.88 us

profile of v1, /device:TPU:1, one launch (start us, length us, event | category | flops | bytes accessed | tf_op | source)
XLA Modules:
  0.0 64.5 jit_solution(16590121228750099821)
XLA Ops:
  0.0 0.7 %fusion.3 = s32[16]{0:T(128)S(1)} fusion(s32[16,1]{0,1:T(1,128)} %param.11, s32[]{:T(128)S(6)} %axis_index.15), kind=kLoop, calls=%fused_computation.11 | loop fusion | flops 128 | bytes 132 | tf_op jit(solution)/shard_map/eq | solution.py:379
  0.7 0.7 %compare_select_fusion.2 = s32[16]{0:T(128)S(1)} fusion(s32[16,1]{0,1:T(1,128)} %param.11, s32[]{:T(128)S(6)} %axis_index.15), kind=kLoop, calls=%fused_computation.7 | loop fusion | flops 128 | bytes 132 | tf_op jit(solution)/shard_map/rem | solution.py:377
  1.3 0.2 convert_reduce_fusion
  1.5 0.7 %multiply_add_fusion.slot_ref = s32[16]{0:T(128)S(1)} fusion(s32[16]{0:T(128)S(1)} %convert_reduce_fusion, s32[16,1]{0,1:T(1,128)} %param.11, s32[]{:T(128)S(6)} %axis_index.15), kind=kLoop, calls=%fused_computation.12 | loop fusion | flops 160 | bytes 196 | tf_op jit(solution)/shard_map/add | solution.py:380
  2.2 0.0 copy-start
  2.2 0.6 select_reduce_fusion.inv_ref
  2.8 1.4 %copy.20.nk_ref = bf16[16,3,256]{2,1,0:T(4,128)(2,1)} copy(bf16[16,3,256]{2,0,1:T(8,128)(2,1)} %param.17) | data formatting | bytes 49152 | tf_op args[7]
  4.2 1.4 %copy.21.nv_ref = bf16[16,3,256]{2,1,0:T(4,128)(2,1)} copy(bf16[16,3,256]{2,0,1:T(8,128)(2,1)} %param.18) | data formatting | bytes 49152 | tf_op args[8]
  5.5 1.0 %copy.23 = bf16[6,8,16,128]{3,2,1,0:T(8,128)(2,1)S(1)} copy(bf16[6,8,16,128]{3,1,2,0:T(8,128)(2,1)} %bitcast.17) | data formatting | bytes 393216
  6.5 0.7 %copy.19.q_ref = bf16[16,3,16,128]{3,2,1,0:T(8,128)(2,1)} copy(bf16[16,3,16,128]{3,2,0,1:T(8,128)(2,1)S(1)} %bitcast.16) | data formatting | bytes 393216 | tf_op jit(solution)/shard_map/reshape | solution.py:431
  7.2 0.0 copy-done
  7.2 55.5 %shard_map.100 = bf16[1,48,2048]{2,1,0:T(8,128)(2,1)} custom-call(s32[16]{0:T(128)} %copy-done, s32[32]{0:T(128)} %select_reduce_fusion.inv_ref, s32[16]{0:T(128)} %len_ref.1, bf16[16,3,16,128]{3,2,1,0:T(8,128)(2,1)} %copy.19.q_ref, bf16[16,3,256]{2,1,0:T(4,128)(2,1)} %copy.20.nk_ref, bf16[16,3,256]{2,1,0:T(4,128)(2,1)} %copy.21.nv_ref, ...), custom_call_target="tpu_custom_call" | custom-call | tf_op jit(solution)/shard_map/pallas_call | solution.py:388
  62.7 1.1 %reshape.30 = bf16[16,3,2048]{2,1,0:T(4,128)(2,1)S(1)} reshape(bf16[1,48,2048]{2,1,0:T(8,128)(2,1)} %shard_map.100) | data formatting | bytes 393216 | tf_op jit(solution)/shard_map/reshape | solution.py:440
  63.7 0.8 %copy.22 = bf16[16,3,2048]{2,0,1:T(8,128)(2,1)} copy(bf16[16,3,2048]{2,1,0:T(4,128)(2,1)S(1)} %reshape.30) | data formatting | bytes 393216 | tf_op jit(solution)/shard_map/reshape | solution.py:440
Async XLA Ops:
  2.2 5.0 %copy-start = (s32[16]{0:T(128)}, s32[16]{0:T(128)S(1)}, u32[]{:S(2)}) copy-start(s32[16]{0:T(128)S(1)} %multiply_add_fusion.slot_ref) | copy-start | bytes 196

commit v2 on v1

v2 whole, which is shorter than its diff:
```python
import functools
import math

import jax
import jax.numpy as jnp
from jax import lax
from jax.experimental import pallas as pl
from jax.experimental.pallas import tpu as pltpu
from jax.sharding import PartitionSpec as P

HD = 128
MESH = pl.DeviceIdType.MESH
NEG = -1e30


def kernel(
    n,
    n_kv,
    cap,
    route_ref,
    len_ref,
    q_ref,
    nk_ref,
    nv_ref,
    pk_hbm,
    pv_hbm,
    sk_hbm,
    sv_hbm,
    w_hbm,
    o_ref,
    kbuf,
    vbuf,
    skbuf,
    svbuf,
    wbuf,
    nkf,
    nvf,
    qx,
    sx,
    sl,
    qsend,
    qrecv,
    psend_o,
    psend_l,
    precv_o,
    precv_l,
    gath,
    ysend,
    red,
    own,
    local_sem,
    q_ss,
    q_rs,
    po_ss,
    po_rs,
    pl_ss,
    pl_rs,
    g_ss,
    g_rs,
    y_ss,
    y_rs,
):
    f32, bf16, i32 = jnp.float32, jnp.bfloat16, jnp.int32
    me = lax.axis_index("dp")
    kv = lax.axis_index("kv")
    rows, width = q_ref.shape
    cands = skbuf.shape[0]
    steps = rows // cands
    heads = width // HD
    kv_heads = kbuf.shape[1] // HD
    group = heads // kv_heads
    gw = group * HD
    pad = nkf.shape[0] // rows
    slots = qsend.shape[2]
    gc = n // n_kv
    cols = wbuf.shape[1]
    scale = 1.0 / math.sqrt(HD)

    loads = [
        pltpu.make_async_copy(src, dst, local_sem.at[i])
        for i, (src, dst) in enumerate(
            [(pk_hbm, kbuf), (pv_hbm, vbuf), (sk_hbm, skbuf), (sv_hbm, svbuf), (w_hbm, wbuf)]
        )
    ]
    for load in loads:
        load.start()

    barrier = pltpu.get_barrier_semaphore()

    @pl.loop(1, n)
    def _(k):
        pl.semaphore_signal(
            barrier, inc=1, device_id={"dp": lax.rem(me + k, n)}, device_id_type=MESH
        )

    @pl.loop(1, n_kv)
    def _(k):
        pl.semaphore_signal(
            barrier, inc=1, device_id={"kv": lax.rem(kv + k, n_kv)}, device_id_type=MESH
        )

    def tables():
        lane = lax.broadcasted_iota(i32, (cands, rows), 1)
        sub = lax.broadcasted_iota(i32, (cands, rows), 0)
        step = jnp.zeros((cands, rows), i32)
        for t in range(1, steps):
            step = step + jnp.where(lane >= t * cands, 1, 0)
        cand = lane - step * cands
        across = jnp.zeros((cands, rows), i32)
        down = jnp.zeros((cands, rows), i32)
        for c in range(cands):
            away = route_ref[c] - me
            away = jnp.where(away < 0, away + n, away)
            across = jnp.where(cand == c, away, across)
            down = jnp.where(sub == c, away, down)
        earlier = jnp.where((across == down) & (sub < cand), 1.0, 0.0)
        rank = jnp.sum(earlier, 0, keepdims=True)
        place = (across * slots + step * cap).astype(f32)[0:1] + rank
        pick = lax.broadcasted_iota(i32, (n * slots, rows), 0).astype(f32) == place
        eye = lax.broadcasted_iota(i32, (rows, rows), 0) == lax.broadcasted_iota(
            i32, (rows, rows), 1
        )
        column = jnp.sum(jnp.where(eye, place, 0.0), 1, keepdims=True)
        back = lax.broadcasted_iota(i32, (rows, n * slots), 1).astype(f32) == column
        return jnp.where(pick, 1.0, 0.0).astype(bf16), jnp.where(back, 1.0, 0.0)

    pick, back = tables()

    def dispatch(h):
        out = jnp.dot(pick, q_ref[:, h * gw : (h + 1) * gw], preferred_element_type=f32)
        for k in range(n):
            part = out[k * slots : (k + 1) * slots].astype(bf16)
            if k == 0:
                qrecv[h, 0] = part
            else:
                qsend[h, k] = part

    def turn(i):
        return 1 + lax.rem(i + n // 2 - 1, n - 1)

    def q_copy(h, k):
        return pltpu.make_async_remote_copy(
            src_ref=qsend.at[h, k],
            dst_ref=qrecv.at[h, k],
            send_sem=q_ss.at[h, k],
            recv_sem=q_rs.at[h, k],
            device_id={"dp": lax.rem(me + k, n)},
            device_id_type=MESH,
        )

    def po_copy(h, k):
        return pltpu.make_async_remote_copy(
            src_ref=psend_o.at[h, k],
            dst_ref=precv_o.at[h, k],
            send_sem=po_ss.at[h, k],
            recv_sem=po_rs.at[h, k],
            device_id={"dp": lax.rem(me + n - k, n)},
            device_id_type=MESH,
        )

    def pl_copy(h, k):
        return pltpu.make_async_remote_copy(
            src_ref=psend_l.at[h, k],
            dst_ref=precv_l.at[h, k],
            send_sem=pl_ss.at[h, k],
            recv_sem=pl_rs.at[h, k],
            device_id={"dp": lax.rem(me + n - k, n)},
            device_id_type=MESH,
        )

    def g_copy(side, h, src):
        to = me + 1 if side == 0 else me - 1
        return pltpu.make_async_remote_copy(
            src_ref=gath.at[h, src],
            dst_ref=gath.at[h, src],
            send_sem=g_ss.at[side, h, src],
            recv_sem=g_rs.at[h, src],
            device_id={"dp": lax.rem(to + n, n)},
            device_id_type=MESH,
        )

    for h in range(kv_heads):
        dispatch(h)
        if h == 0:
            pl.semaphore_wait(barrier, n - 1 + n_kv - 1)

        @pl.loop(0, n - 1)
        def _(i):
            q_copy(h, turn(i)).start()

    for hg in range(heads):
        qx[pl.ds(hg, rows, stride=heads), :] = q_ref[:, hg * HD : (hg + 1) * HD].astype(f32)
    for h in range(kv_heads):
        nkf[pl.ds(h, rows, stride=pad), :] = nk_ref[:, h * HD : (h + 1) * HD].astype(f32)
        nvf[pl.ds(h, rows, stride=pad), :] = nv_ref[:, h * HD : (h + 1) * HD].astype(f32)

    lane = lax.broadcasted_iota(i32, (slots, HD), 1)

    def attend(h, k):
        x = qrecv[h, k].astype(f32)
        x = jnp.concatenate([x[:, g * HD : (g + 1) * HD] for g in range(group)], 0)
        lanes = slice(h * HD, (h + 1) * HD)
        s = (
            lax.dot_general(
                x.astype(bf16),
                kbuf[:, lanes],
                (((1,), (1,)), ((), ())),
                preferred_element_type=f32,
            )
            * scale
        )
        top = jnp.max(s, 1, keepdims=True)
        p = jnp.exp(s - top)
        total = jnp.sum(p, 1, keepdims=True)
        o = jnp.dot(p.astype(bf16), vbuf[:, lanes], preferred_element_type=f32) / total
        lse = jnp.broadcast_to(top + jnp.log(total), (slots * group, HD))
        packed = jnp.zeros((slots, HD), f32)
        for g in range(group):
            packed = jnp.where(lane == g, lse[g * slots : (g + 1) * slots], packed)
        o = jnp.concatenate([o[g * slots : (g + 1) * slots] for g in range(group)], 1)
        return o.astype(bf16), packed

    depth = skbuf.shape[1]
    position = lax.broadcasted_iota(i32, (steps * group, depth), 1)
    row_of = lax.broadcasted_iota(i32, (steps * group, 1), 0)

    def suffix(c):
        length = len_ref[c]
        news_at = [
            pl.ds(pl.multiple_of((t * cands + c) * pad, 8), pad) for t in range(steps)
        ]
        for h in range(kv_heads):
            lanes = slice(h * HD, (h + 1) * HD)
            places = [
                pl.ds(pl.multiple_of((t * cands + c) * heads + h * group, 8), group)
                for t in range(steps)
            ]
            qh = jnp.concatenate([qx[place, :] for place in places], 0)
            s = lax.dot_general(
                qh.astype(bf16),
                skbuf[c, :, lanes],
                (((1,), (1,)), ((), ())),
                preferred_element_type=f32,
            )
            s = jnp.where(position < length, s * scale, NEG)
            top = jnp.max(s, 1, keepdims=True)
            news = []
            for t in range(steps):
                fresh = nkf[news_at[t], :][h : h + 1]
                f = jnp.sum(qh * fresh, 1, keepdims=True) * scale
                f = jnp.where(row_of >= t * group, f, NEG)
                top = jnp.maximum(top, f)
                news.append(f)
            p = jnp.exp(s - top)
            total = jnp.sum(p, 1, keepdims=True)
            o = jnp.dot(p.astype(bf16), svbuf[c, :, lanes], preferred_element_type=f32)
            for t in range(steps):
                e = jnp.exp(news[t] - top)
                total = total + e
                o = o + e * nvf[news_at[t], :][h : h + 1]
            o = o / total
            lse = jnp.broadcast_to(top + jnp.log(total), (steps * group, HD))
            for t, place in enumerate(places):
                sx[place, :] = o[t * group : (t + 1) * group]
                sl[place, :] = lse[t * group : (t + 1) * group]

    together = 4 if cands % 8 == 0 else 1
    half = cands // together // 2

    loads[0].wait()
    loads[1].wait()
    for h in range(kv_heads):
        o, packed = attend(h, 0)
        precv_o[h, 0] = o
        precv_l[h, 0] = packed
    loads[2].wait()
    loads[3].wait()

    @pl.loop(0, half)
    def _(i):
        for u in range(together):
            suffix(i * together + u)

    for h in range(kv_heads):

        @pl.loop(0, n - 1)
        def _(i):
            k = turn(i)
            q_copy(h, k).wait_recv()
            o, packed = attend(h, k)
            psend_o[h, k] = o
            psend_l[h, k] = packed
            po_copy(h, k).start()
            pl_copy(h, k).start()

    @pl.loop(half, cands // together)
    def _(i):
        for u in range(together):
            suffix(i * together + u)

    for h in range(kv_heads):

        @pl.loop(1, n)
        def _(k):
            po_copy(h, k).wait_recv()
            pl_copy(h, k).wait_recv()

        prompt = precv_o[h].astype(f32).reshape(n * slots, gw).astype(bf16)
        prompt = jnp.dot(back.astype(bf16), prompt, preferred_element_type=f32)
        totals = jnp.dot(
            back,
            precv_l[h].reshape(n * slots, HD),
            preferred_element_type=f32,
            precision=lax.Precision.HIGHEST,
        )
        for g in range(group):
            spot = pl.ds(h * group + g, rows, stride=heads)
            pt = totals[:, g : g + 1]
            st = sl[spot, :]
            peak = jnp.maximum(pt, st)
            a = jnp.exp(pt - peak)
            b = jnp.exp(st - peak)
            merged = (a * prompt[:, g * HD : (g + 1) * HD] + b * sx[spot, :]) / (a + b)
            gath[h, me, :, g * HD : (g + 1) * HD] = merged.astype(bf16)

        @pl.when(me < n - 1)
        def _():
            g_copy(0, h, me).start()

        @pl.when(me > 0)
        def _():
            g_copy(1, h, me).start()

    loads[4].wait()
    tile = min(512, cols)

    def y_copy(src):
        to = src // gc
        j = lax.rem(to + n_kv - kv, n_kv)
        pos = lax.rem(src, gc)
        return j, pos, pltpu.make_async_remote_copy(
            src_ref=ysend.at[src],
            dst_ref=red.at[j, pos],
            send_sem=y_ss.at[src],
            recv_sem=y_rs.at[j, pos],
            device_id={"kv": to},
            device_id_type=MESH,
        )

    def project(src):
        j, pos, copy = y_copy(src)

        @pl.loop(0, cols // tile)
        def _(t):
            at = pl.ds(pl.multiple_of(t * tile, 128), tile)
            y = jnp.dot(gath[0, src], wbuf[0:gw, at], preferred_element_type=f32)
            for h in range(1, kv_heads):
                y = y + jnp.dot(
                    gath[h, src], wbuf[h * gw : (h + 1) * gw, at], preferred_element_type=f32
                )

            @pl.when(j == 0)
            def _():
                own[pos, :, at] = y

            @pl.when(j > 0)
            def _():
                ysend[src, :, at] = y.astype(bf16)

        @pl.when(j > 0)
        def _():
            copy.start()

    project(me)

    @pl.loop(1, n)
    def _(d):
        before, after = me - d, me + d
        for h in range(kv_heads):

            @pl.when(before >= 0)
            def _():
                g_copy(0, h, before).wait_recv()

                @pl.when(me < n - 1)
                def _():
                    g_copy(0, h, before).start()

            @pl.when(after < n)
            def _():
                g_copy(1, h, after).wait_recv()

                @pl.when(me > 0)
                def _():
                    g_copy(1, h, after).start()

        @pl.loop(0, 2)
        def _(side):
            src = jnp.where(side == 0, before, after)

            @pl.when((src >= 0) & (src < n))
            def _():
                project(src)

    @pl.loop(0, gc)
    def _(pos):
        total = own[pos]
        for j in range(1, n_kv):
            pltpu.make_async_remote_copy(
                src_ref=ysend.at[0],
                dst_ref=red.at[j, pos],
                send_sem=y_ss.at[0],
                recv_sem=y_rs.at[j, pos],
                device_id={"kv": lax.rem(kv + j, n_kv)},
                device_id_type=MESH,
            ).wait_recv()
            total = total + red[j, pos].astype(f32)
        o_ref[pos] = total.astype(bf16)

    for h in range(kv_heads):

        @pl.loop(1, n)
        def _(k):
            q_copy(h, k).wait_send()
            po_copy(h, k).wait_send()
            pl_copy(h, k).wait_send()

        @pl.loop(0, n)
        def _(src):
            @pl.when((src <= me) & (me < n - 1))
            def _():
                g_copy(0, h, src).wait_send()

            @pl.when((src >= me) & (me > 0))
            def _():
                g_copy(1, h, src).wait_send()

    @pl.loop(0, n)
    def _(src):
        j, pos, copy = y_copy(src)

        @pl.when(j > 0)
        def _():
            copy.wait_send()


def local(
    queries,
    routes,
    suffix_lengths,
    prefix_keys,
    prefix_values,
    suffix_keys,
    suffix_values,
    new_keys,
    new_values,
    out_weight,
):
    n = lax.axis_size("dp")
    n_kv = lax.axis_size("kv")
    cands, steps, query_width = queries.shape
    kv_width = prefix_keys.shape[2]
    plen = prefix_keys.shape[1]
    depth = suffix_keys.shape[1]
    cols = out_weight.shape[1]
    heads = query_width // HD
    kv_heads = kv_width // HD
    gw = query_width // kv_heads
    rows = cands * steps
    gc = n // n_kv
    cap = max(2, 2 * cands // n)
    slots = -(-cap * steps // 8) * 8
    pad = -(-kv_heads // 8) * 8
    bf16, f32 = jnp.bfloat16, jnp.float32
    smem = pl.BlockSpec(memory_space=pltpu.SMEM)
    vmem = pl.BlockSpec(memory_space=pltpu.VMEM)
    hbm = pl.BlockSpec(memory_space=pl.ANY)
    dma = pltpu.SemaphoreType.DMA

    def by_step(x):
        return jnp.transpose(x, (1, 0, 2)).reshape(rows, x.shape[2])

    out = pl.pallas_call(
        functools.partial(kernel, n, n_kv, cap),
        out_shape=jax.ShapeDtypeStruct((gc, rows, cols), bf16),
        in_specs=[smem] * 2 + [vmem] * 3 + [hbm] * 5,
        out_specs=vmem,
        scratch_shapes=[
            pltpu.VMEM((plen, kv_width), bf16),
            pltpu.VMEM((plen, kv_width), bf16),
            pltpu.VMEM((cands, depth, kv_width), bf16),
            pltpu.VMEM((cands, depth, kv_width), bf16),
            pltpu.VMEM((query_width, cols), bf16),
            pltpu.VMEM((rows * pad, HD), f32),
            pltpu.VMEM((rows * pad, HD), f32),
            pltpu.VMEM((rows * heads, HD), f32),
            pltpu.VMEM((rows * heads, HD), f32),
            pltpu.VMEM((rows * heads, HD), f32),
            pltpu.VMEM((kv_heads, n, slots, gw), bf16),
            pltpu.VMEM((kv_heads, n, slots, gw), bf16),
            pltpu.VMEM((kv_heads, n, slots, gw), bf16),
            pltpu.VMEM((kv_heads, n, slots, HD), f32),
            pltpu.VMEM((kv_heads, n, slots, gw), bf16),
            pltpu.VMEM((kv_heads, n, slots, HD), f32),
            pltpu.VMEM((kv_heads, n, rows, gw), bf16),
            pltpu.VMEM((n, rows, cols), bf16),
            pltpu.VMEM((n_kv, gc, rows, cols), bf16),
            pltpu.VMEM((gc, rows, cols), f32),
            dma((5,)),
            dma((kv_heads, n)),
            dma((kv_heads, n)),
            dma((kv_heads, n)),
            dma((kv_heads, n)),
            dma((kv_heads, n)),
            dma((kv_heads, n)),
            dma((2, kv_heads, n)),
            dma((kv_heads, n)),
            dma((n,)),
            dma((n_kv, gc)),
        ],
        compiler_params=pltpu.CompilerParams(
            collective_id=0, has_side_effects=True, vmem_limit_bytes=60 * 1024 * 1024
        ),
    )(
        routes.reshape(cands),
        suffix_lengths,
        by_step(queries),
        by_step(new_keys),
        by_step(new_values),
        prefix_keys[0],
        prefix_values[0],
        suffix_keys,
        suffix_values,
        out_weight,
    )
    out = jnp.transpose(out.reshape(gc, steps, cands, cols), (0, 2, 1, 3))
    return out.reshape(gc * cands, steps, cols)


def solution(mesh):
    placed = (
        P(("groups", "dp"), None, "kv"),
        P(("groups", "dp"), None),
        P(("groups", "dp")),
        P(("groups", "dp"), None, "kv"),
        P(("groups", "dp"), None, "kv"),
        P(("groups", "dp"), None, "kv"),
        P(("groups", "dp"), None, "kv"),
        P(("groups", "dp"), None, "kv"),
        P(("groups", "dp"), None, "kv"),
        P("kv", "dp"),
    )
    return jax.shard_map(
        local,
        mesh=mesh,
        in_specs=placed,
        out_specs=P(("groups", "kv"), None, "dp"),
        check_vma=False,
    )
```

time: 64.9 us -> 48.2 us (0.74)
  the two profiles are of different devices: /device:TPU:1 before, /device:TPU:0 now
where the time goes in v2:
time: 48.2 us; the launch traced here: 48.1 us
  Pallas kernels  46.5 us (96%)
  local copies, waits for them, and re-layouts  1.62 us (3%)
    pallas_call x1, Pallas kernels, local(): pl.pallas_call(functools.partial(kernel, n, n_kv, cap), out_shape=jax.Sha...  46.5 us
    unnamed x1, local copies, waits for them, and re-layouts  1.62 us

profile of v2, /device:TPU:0, one launch (start us, length us, event | category | flops | bytes accessed | tf_op | source)
XLA Modules:
  0.0 48.1 jit_solution(13433188247515411589)
XLA Ops:
  0.0 46.5 %shard_map.100 = bf16[1,48,2048]{2,1,0:T(8,128)(2,1)} custom-call(s32[16]{0:T(128)} %bitcast.23, s32[16]{0:T(128)} %len_ref.1, bf16[48,2048]{1,0:T(8,128)(2,1)} %bitcast.20, bf16[48,256]{1,0:T(8,128)(2,1)} %bitcast.21, bf16[48,256]{1,0:T(8,128)(2,1)} %bitcast.22, bf16[2048,256]{1,0:T(8,128)(2,1)} %bitcast.17, bf16[2048,256]{1,0:T(8,128)(2,1)} %bitcast.18, ...), custom_call_target="tpu_custom_call" | custom-call | tf_op jit(solution)/shard_map/pallas_call | solution.py:483
  46.5 1.6 %copy.12 = bf16[16,3,2048]{2,0,1:T(8,128)(2,1)} copy(bf16[16,3,2048]{2,0,1:T(8,128)(2,1)} %bitcast.19) | data formatting | bytes 393216

commit v3 on v2

--- a/solution.py
+++ b/solution.py
@@ -179,14 +179,16 @@
             device_id_type=MESH,
         )
 
-    for h in range(kv_heads):
-        dispatch(h)
-        if h == 0:
-            pl.semaphore_wait(barrier, n - 1 + n_kv - 1)
-
+    def ask(h):
         @pl.loop(0, n - 1)
         def _(i):
             q_copy(h, turn(i)).start()
+
+    dispatch(0)
+    pl.semaphore_wait(barrier, n - 1 + n_kv - 1)
+    ask(0)
+    for h in range(1, kv_heads):
+        dispatch(h)
 
     for hg in range(heads):
         qx[pl.ds(hg, rows, stride=heads), :] = q_ref[:, hg * HD : (hg + 1) * HD].astype(f32)
@@ -194,7 +196,8 @@
         nkf[pl.ds(h, rows, stride=pad), :] = nk_ref[:, h * HD : (h + 1) * HD].astype(f32)
         nvf[pl.ds(h, rows, stride=pad), :] = nv_ref[:, h * HD : (h + 1) * HD].astype(f32)
 
-    lane = lax.broadcasted_iota(i32, (slots, HD), 1)
+    tiles = slots // 8
+    lane = lax.broadcasted_iota(i32, (8, HD), 1)
 
     def attend(h, k):
         x = qrecv[h, k].astype(f32)
@@ -214,9 +217,11 @@
         total = jnp.sum(p, 1, keepdims=True)
         o = jnp.dot(p.astype(bf16), vbuf[:, lanes], preferred_element_type=f32) / total
         lse = jnp.broadcast_to(top + jnp.log(total), (slots * group, HD))
-        packed = jnp.zeros((slots, HD), f32)
+        packed = jnp.zeros((8, HD), f32)
         for g in range(group):
-            packed = jnp.where(lane == g, lse[g * slots : (g + 1) * slots], packed)
+            for t in range(tiles):
+                at = g * slots + t * 8
+                packed = jnp.where(lane == t * group + g, lse[at : at + 8], packed)
         o = jnp.concatenate([o[g * slots : (g + 1) * slots] for g in range(group)], 1)
         return o.astype(bf16), packed
 
@@ -224,65 +229,59 @@
     position = lax.broadcasted_iota(i32, (steps * group, depth), 1)
     row_of = lax.broadcasted_iota(i32, (steps * group, 1), 0)
 
-    def suffix(c):
+    def suffix(h, c):
         length = len_ref[c]
         news_at = [
             pl.ds(pl.multiple_of((t * cands + c) * pad, 8), pad) for t in range(steps)
         ]
-        for h in range(kv_heads):
-            lanes = slice(h * HD, (h + 1) * HD)
-            places = [
-                pl.ds(pl.multiple_of((t * cands + c) * heads + h * group, 8), group)
-                for t in range(steps)
-            ]
-            qh = jnp.concatenate([qx[place, :] for place in places], 0)
-            s = lax.dot_general(
-                qh.astype(bf16),
-                skbuf[c, :, lanes],
-                (((1,), (1,)), ((), ())),
-                preferred_element_type=f32,
-            )
-            s = jnp.where(position < length, s * scale, NEG)
-            top = jnp.max(s, 1, keepdims=True)
-            news = []
-            for t in range(steps):
-                fresh = nkf[news_at[t], :][h : h + 1]
-                f = jnp.sum(qh * fresh, 1, keepdims=True) * scale
-                f = jnp.where(row_of >= t * group, f, NEG)
-                top = jnp.maximum(top, f)
-                news.append(f)
-            p = jnp.exp(s - top)
-            total = jnp.sum(p, 1, keepdims=True)
-            o = jnp.dot(p.astype(bf16), svbuf[c, :, lanes], preferred_element_type=f32)
-            for t in range(steps):
-                e = jnp.exp(news[t] - top)
-                total = total + e
-                o = o + e * nvf[news_at[t], :][h : h + 1]
-            o = o / total
-            lse = jnp.broadcast_to(top + jnp.log(total), (steps * group, HD))
-            for t, place in enumerate(places):
-                sx[place, :] = o[t * group : (t + 1) * group]
-                sl[place, :] = lse[t * group : (t + 1) * group]
-
-    together = 4 if cands % 8 == 0 else 1
-    half = cands // together // 2
-
-    loads[0].wait()
-    loads[1].wait()
-    for h in range(kv_heads):
+        lanes = slice(h * HD, (h + 1) * HD)
+        places = [
+            pl.ds(pl.multiple_of((t * cands + c) * heads + h * group, 8), group)
+            for t in range(steps)
+        ]
+        qh = jnp.concatenate([qx[place, :] for place in places], 0)
+        s = lax.dot_general(
+            qh.astype(bf16),
+            skbuf[c, :, lanes],
+            (((1,), (1,)), ((), ())),
+            preferred_element_type=f32,
+        )
+        s = jnp.where(position < length, s * scale, NEG)
+        top = jnp.max(s, 1, keepdims=True)
+        news = []
+        for t in range(steps):
+            fresh = nkf[news_at[t], :][h : h + 1]
+            f = jnp.sum(qh * fresh, 1, keepdims=True) * scale
+            f = jnp.where(row_of >= t * group, f, NEG)
+            top = jnp.maximum(top, f)
+            news.append(f)
+        p = jnp.exp(s - top)
+        total = jnp.sum(p, 1, keepdims=True)
+        o = jnp.dot(p.astype(bf16), svbuf[c, :, lanes], preferred_element_type=f32)
+        for t in range(steps):
+            e = jnp.exp(news[t] - top)
+            total = total + e
+            o = o + e * nvf[news_at[t], :][h : h + 1]
+        o = o / total
+        lse = jnp.broadcast_to(top + jnp.log(total), (steps * group, HD))
+        for t, place in enumerate(places):
+            sx[place, :] = o[t * group : (t + 1) * group]
+            sl[place, :] = lse[t * group : (t + 1) * group]
+
+    together = 8 if cands % 8 == 0 else 1
+
+    def suffixes(h):
+        @pl.loop(0, cands // together)
+        def _(i):
+            for u in range(together):
+                suffix(h, i * together + u)
+
+    def here(h):
         o, packed = attend(h, 0)
         precv_o[h, 0] = o
         precv_l[h, 0] = packed
-    loads[2].wait()
-    loads[3].wait()
-
-    @pl.loop(0, half)
-    def _(i):
-        for u in range(together):
-            suffix(i * together + u)
-
-    for h in range(kv_heads):
-
+
+    def serve(h):
         @pl.loop(0, n - 1)
         def _(i):
             k = turn(i)
@@ -290,16 +289,10 @@
             o, packed = attend(h, k)
             psend_o[h, k] = o
             psend_l[h, k] = packed
+            pl_copy(h, k).start()
             po_copy(h, k).start()
-            pl_copy(h, k).start()
-
-    @pl.loop(half, cands // together)
-    def _(i):
-        for u in range(together):
-            suffix(i * together + u)
-
-    for h in range(kv_heads):
-
+
+    def merge(h):
         @pl.loop(1, n)
         def _(k):
             po_copy(h, k).wait_recv()
@@ -307,15 +300,26 @@
 
         prompt = precv_o[h].astype(f32).reshape(n * slots, gw).astype(bf16)
         prompt = jnp.dot(back.astype(bf16), prompt, preferred_element_type=f32)
+        wide = lax.broadcasted_iota(i32, (n, 8, HD), 2)
+        packed = precv_l[h]
+        spread = jnp.concatenate(
+            [
+                jnp.where((wide >= t * group) & (wide < (t + 1) * group), packed, 0.0)[:, None]
+                for t in range(tiles)
+            ],
+            1,
+        ).reshape(n * slots, HD)
         totals = jnp.dot(
             back,
-            precv_l[h].reshape(n * slots, HD),
+            spread,
             preferred_element_type=f32,
             precision=lax.Precision.HIGHEST,
         )
         for g in range(group):
             spot = pl.ds(h * group + g, rows, stride=heads)
             pt = totals[:, g : g + 1]
+            for t in range(1, tiles):
+                pt = pt + totals[:, t * group + g : t * group + g + 1]
             st = sl[spot, :]
             peak = jnp.maximum(pt, st)
             a = jnp.exp(pt - peak)
@@ -331,27 +335,68 @@
         def _():
             g_copy(1, h, me).start()
 
+    def relay(h, d):
+        before, after = me - d, me + d
+
+        @pl.when(before >= 0)
+        def _():
+            g_copy(0, h, before).wait_recv()
+
+            @pl.when(me < n - 1)
+            def _():
+                g_copy(0, h, before).start()
+
+        @pl.when(after < n)
+        def _():
+            g_copy(1, h, after).wait_recv()
+
+            @pl.when(me > 0)
+            def _():
+                g_copy(1, h, after).start()
+
+    loads[0].wait()
+    loads[1].wait()
+    here(0)
+    serve(0)
+    for h in range(kv_heads):
+        if h + 1 < kv_heads:
+            ask(h + 1)
+        if h == 0:
+            loads[2].wait()
+            loads[3].wait()
+            suffixes(h)
+        merge(h)
+        if h + 1 < kv_heads:
+            here(h + 1)
+            suffixes(h + 1)
+            relay(h, 1)
+            serve(h + 1)
+
+            @pl.loop(2, n)
+            def _(d):
+                relay(h, d)
+
     loads[4].wait()
     tile = min(512, cols)
 
-    def y_copy(src):
+    def y_copy(src, t):
         to = src // gc
         j = lax.rem(to + n_kv - kv, n_kv)
         pos = lax.rem(src, gc)
+        at = pl.ds(pl.multiple_of(t * tile, 128), tile)
         return j, pos, pltpu.make_async_remote_copy(
-            src_ref=ysend.at[src],
-            dst_ref=red.at[j, pos],
-            send_sem=y_ss.at[src],
-            recv_sem=y_rs.at[j, pos],
+            src_ref=ysend.at[src, :, at],
+            dst_ref=red.at[j, pos, :, at],
+            send_sem=y_ss.at[src, t],
+            recv_sem=y_rs.at[j, pos, t],
             device_id={"kv": to},
             device_id_type=MESH,
         )
 
     def project(src):
-        j, pos, copy = y_copy(src)
-
         @pl.loop(0, cols // tile)
         def _(t):
+            j, pos, copy = y_copy(src, t)
             at = pl.ds(pl.multiple_of(t * tile, 128), tile)
             y = jnp.dot(gath[0, src], wbuf[0:gw, at], preferred_element_type=f32)
             for h in range(1, kv_heads):
@@ -366,37 +411,17 @@
             @pl.when(j > 0)
             def _():
                 ysend[src, :, at] = y.astype(bf16)
-
-        @pl.when(j > 0)
-        def _():
-            copy.start()
+                copy.start()
 
     project(me)
 
     @pl.loop(1, n)
     def _(d):
-        before, after = me - d, me + d
-        for h in range(kv_heads):
-
-            @pl.when(before >= 0)
-            def _():
-                g_copy(0, h, before).wait_recv()
-
-                @pl.when(me < n - 1)
-                def _():
-                    g_copy(0, h, before).start()
-
-            @pl.when(after < n)
-            def _():
-                g_copy(1, h, after).wait_recv()
-
-                @pl.when(me > 0)
-                def _():
-                    g_copy(1, h, after).start()
+        relay(kv_heads - 1, d)
 
         @pl.loop(0, 2)
         def _(side):
-            src = jnp.where(side == 0, before, after)
+            src = jnp.where(side == 0, me - d, me + d)
 
             @pl.when((src >= 0) & (src < n))
             def _():
@@ -404,18 +429,21 @@
 
     @pl.loop(0, gc)
     def _(pos):
-        total = own[pos]
-        for j in range(1, n_kv):
-            pltpu.make_async_remote_copy(
-                src_ref=ysend.at[0],
-                dst_ref=red.at[j, pos],
-                send_sem=y_ss.at[0],
-                recv_sem=y_rs.at[j, pos],
-                device_id={"kv": lax.rem(kv + j, n_kv)},
-                device_id_type=MESH,
-            ).wait_recv()
-            total = total + red[j, pos].astype(f32)
-        o_ref[pos] = total.astype(bf16)
+        @pl.loop(0, cols // tile)
+        def _(t):
+            at = pl.ds(pl.multiple_of(t * tile, 128), tile)
+            total = own[pos, :, at]
+            for j in range(1, n_kv):
+                pltpu.make_async_remote_copy(
+                    src_ref=ysend.at[0, :, at],
+                    dst_ref=red.at[j, pos, :, at],
+                    send_sem=y_ss.at[0, t],
+                    recv_sem=y_rs.at[j, pos, t],
+                    device_id={"kv": lax.rem(kv + j, n_kv)},
+                    device_id_type=MESH,
+                ).wait_recv()
+                total = total + red[j, pos, :, at].astype(f32)
+            o_ref[pos, :, at] = total.astype(bf16)
 
     for h in range(kv_heads):
 
@@ -437,11 +465,13 @@
 
     @pl.loop(0, n)
     def _(src):
-        j, pos, copy = y_copy(src)
-
-        @pl.when(j > 0)
-        def _():
-            copy.wait_send()
+        @pl.loop(0, cols // tile)
+        def _(t):
+            j, pos, copy = y_copy(src, t)
+
+            @pl.when(j > 0)
+            def _():
+                copy.wait_send()
 
 
 def local(
@@ -499,9 +529,9 @@
             pltpu.VMEM((kv_heads, n, slots, gw), bf16),
             pltpu.VMEM((kv_heads, n, slots, gw), bf16),
             pltpu.VMEM((kv_heads, n, slots, gw), bf16),
-            pltpu.VMEM((kv_heads, n, slots, HD), f32),
+            pltpu.VMEM((kv_heads, n, 8, HD), f32),
             pltpu.VMEM((kv_heads, n, slots, gw), bf16),
-            pltpu.VMEM((kv_heads, n, slots, HD), f32),
+            pltpu.VMEM((kv_heads, n, 8, HD), f32),
             pltpu.VMEM((kv_heads, n, rows, gw), bf16),
             pltpu.VMEM((n, rows, cols), bf16),
             pltpu.VMEM((n_kv, gc, rows, cols), bf16),
@@ -515,8 +545,8 @@
             dma((kv_heads, n)),
             dma((2, kv_heads, n)),
             dma((kv_heads, n)),
-            dma((n,)),
-            dma((n_kv, gc)),
+            dma((n, cols // min(512, cols))),
+            dma((n_kv, gc, cols // min(512, cols))),
         ],
         compiler_params=pltpu.CompilerParams(
             collective_id=0, has_side_effects=True, vmem_limit_bytes=60 * 1024 * 1024

time: 48.2 us -> 51.9 us (1.077)
  Pallas kernels: 46.5 us -> 50.1 us
    pallas_call x1, Pallas kernels: 46.5 us -> 50.1 us  [local(): pl.pallas_call(functools.partial(kernel, n, n_kv, cap), out_shape=jax.Sha...]
where the time goes in v3:
time: 51.9 us; the launch traced here: 51.8 us
  Pallas kernels  50.1 us (97%)
  local copies, waits for them, and re-layouts  1.62 us (3%)
    pallas_call x1, Pallas kernels, local(): pl.pallas_call(functools.partial(kernel, n, n_kv, cap), out_shape=jax.Sha...  50.1 us
    unnamed x1, local copies, waits for them, and re-layouts  1.62 us

profile of v3, /device:TPU:0, one launch (start us, length us, event | category | flops | bytes accessed | tf_op | source)
XLA Modules:
  0.0 51.8 jit_solution(11669813790746903289)
XLA Ops:
  0.0 50.1 %shard_map.100 = bf16[1,48,2048]{2,1,0:T(8,128)(2,1)} custom-call(s32[16]{0:T(128)} %bitcast.23, s32[16]{0:T(128)} %len_ref.1, bf16[48,2048]{1,0:T(8,128)(2,1)} %bitcast.20, bf16[48,256]{1,0:T(8,128)(2,1)} %bitcast.21, bf16[48,256]{1,0:T(8,128)(2,1)} %bitcast.22, bf16[2048,256]{1,0:T(8,128)(2,1)} %bitcast.17, bf16[2048,256]{1,0:T(8,128)(2,1)} %bitcast.18, ...), custom_call_target="tpu_custom_call" | custom-call | tf_op jit(solution)/shard_map/pallas_call | solution.py:513
  50.1 1.6 %copy.12 = bf16[16,3,2048]{2,0,1:T(8,128)(2,1)} copy(bf16[16,3,2048]{2,0,1:T(8,128)(2,1)} %bitcast.19) | data formatting | bytes 393216

commit v4 on v3

--- a/solution.py
+++ b/solution.py
@@ -136,7 +136,7 @@
                 qsend[h, k] = part
 
     def turn(i):
-        return 1 + lax.rem(i + n // 2 - 1, n - 1)
+        return 1 + i
 
     def q_copy(h, k):
         return pltpu.make_async_remote_copy(
@@ -189,6 +189,7 @@
     ask(0)
     for h in range(1, kv_heads):
         dispatch(h)
+        ask(h)
 
     for hg in range(heads):
         qx[pl.ds(hg, rows, stride=heads), :] = q_ref[:, hg * HD : (hg + 1) * HD].astype(f32)
@@ -356,25 +357,17 @@
 
     loads[0].wait()
     loads[1].wait()
-    here(0)
-    serve(0)
     for h in range(kv_heads):
-        if h + 1 < kv_heads:
-            ask(h + 1)
-        if h == 0:
-            loads[2].wait()
-            loads[3].wait()
-            suffixes(h)
+        here(h)
+    loads[2].wait()
+    loads[3].wait()
+    suffixes(0)
+    for h in range(kv_heads):
+        serve(h)
+    for h in range(1, kv_heads):
+        suffixes(h)
+    for h in range(kv_heads):
         merge(h)
-        if h + 1 < kv_heads:
-            here(h + 1)
-            suffixes(h + 1)
-            relay(h, 1)
-            serve(h + 1)
-
-            @pl.loop(2, n)
-            def _(d):
-                relay(h, d)
 
     loads[4].wait()
     tile = min(512, cols)
@@ -417,7 +410,8 @@
 
     @pl.loop(1, n)
     def _(d):
-        relay(kv_heads - 1, d)
+        for h in range(kv_heads):
+            relay(h, d)
 
         @pl.loop(0, 2)
         def _(side):

time: 51.9 us -> 45.2 us (0.87)
  Pallas kernels: 50.1 us -> 43.4 us
    pallas_call x1, Pallas kernels: 50.1 us -> 43.4 us  [local(): pl.pallas_call(functools.partial(kernel, n, n_kv, cap), out_shape=jax.Sha...]
where the time goes in v4:
time: 45.2 us; the launch traced here: 45 us
  Pallas kernels  43.4 us (96%)
  local copies, waits for them, and re-layouts  1.62 us (4%)
    pallas_call x1, Pallas kernels, local(): pl.pallas_call(functools.partial(kernel, n, n_kv, cap), out_shape=jax.Sha...  43.4 us
    unnamed x1, local copies, waits for them, and re-layouts  1.62 us

profile of v4, /device:TPU:0, one launch (start us, length us, event | category | flops | bytes accessed | tf_op | source)
XLA Modules:
  0.0 45.0 jit_solution(4564364305355738879)
XLA Ops:
  0.0 43.4 %shard_map.100 = bf16[1,48,2048]{2,1,0:T(8,128)(2,1)} custom-call(s32[16]{0:T(128)} %bitcast.23, s32[16]{0:T(128)} %len_ref.1, bf16[48,2048]{1,0:T(8,128)(2,1)} %bitcast.20, bf16[48,256]{1,0:T(8,128)(2,1)} %bitcast.21, bf16[48,256]{1,0:T(8,128)(2,1)} %bitcast.22, bf16[2048,256]{1,0:T(8,128)(2,1)} %bitcast.17, bf16[2048,256]{1,0:T(8,128)(2,1)} %bitcast.18, ...), custom_call_target="tpu_custom_call" | custom-call | tf_op jit(solution)/shard_map/pallas_call | solution.py:507
  43.4 1.6 %copy.12 = bf16[16,3,2048]{2,0,1:T(8,128)(2,1)} copy(bf16[16,3,2048]{2,0,1:T(8,128)(2,1)} %bitcast.19) | data formatting | bytes 393216
